TPU v7x, 256 devices: a whole 4x4x8 slice. The times are simulated.
256 devices in a mesh: dp: 16 (over z, x_lo), seq: 16 (over y, x_hi, core).
Axes of the slice: x: 4 (x_hi: 2, x_lo: 2; x = x_hi * 2 + x_lo), y: 4, z: 8, core: 2. Of those that a mesh axis runs over, the one named last changes fastest.
Arguments:
- frames: bfloat16 [16, 4096, 1536], P('dp', 'seq'), may hold values from -0.29882812 to 0.29882812
- segment_ids: int32 [16, 4096], P('dp', 'seq'), may hold values from 0 to 11, never falling along the last dimension, each value on 1 to 3072 neighbouring positions
- ln_attn_gain: float32 [1536], replicated, may hold values from 0.25 to 1.75
- w_qkv: bfloat16 [1536, 2304], P('dp'), as said below
- w_out: bfloat16 [768, 1536], P('dp'), may hold values from -0.21875 to 0.21875
- ln_conv_gain: float32 [1536], replicated, may hold values from 0.25 to 1.75
- w_glu: bfloat16 [1536, 3072], P('dp'), may hold values from -0.15625 to 0.15625
- dw_kernel: float32 [32, 1536], replicated, may hold values from -1 to 1
- ln_mid_gain: float32 [1536], replicated, may hold values from 0.25 to 1.75
Outputs:
- block_out: bfloat16 [16, 4096, 1536], P('dp', 'seq')
Inputs may be any that keep to these rules, and one draw needn't show every extreme that they name: `segment_ids`: within each stream the ids start at 0 and never fall; each utterance has 1 to 3072 frames and one has exactly 3072. `w_qkv`: a projection matrix with independent entries.
All inputs are finite; a program needn't handle non-finite values.
Results may differ from a plain program's by a relative error of at most 0.025.
The roundings to bfloat16 on the way count: a program that leaves them out, or rounds other values in their place, can miss the bound.
Values may be sent and summed in bfloat16 or wider, within the bound.
No kernel may reach another device: no remote copies, remote signals or barrier semaphores. Data moves between devices by JAX's collectives and lax.ppermute only.
A program may use at most 192 MiB of HBM per device.

v0:
```python
import math
import jax
import jax.numpy as jnp
from jax import lax
from jax.sharding import PartitionSpec as P

D = 1536
HEADS = 12
HD = 64
CONV_K = 32


def with_halo(block, sides, width):
    for axis, dim in sides:
        count = lax.axis_size(axis)
        forward = [(i, i + 1) for i in range(count - 1)]
        backward = [(target, source) for source, target in forward]
        low = lax.ppermute(
            lax.slice_in_dim(block, block.shape[dim] - width, None, axis=dim), axis, forward
        )
        high = lax.ppermute(lax.slice_in_dim(block, 0, width, axis=dim), axis, backward)
        block = jnp.concatenate([low, block, high], axis=dim)
    return block


def layer_norm(values, gain):
    values = values.astype(jnp.float32)
    centre = jnp.mean(values, -1, keepdims=True)
    spread = jnp.mean((values - centre) ** 2, -1, keepdims=True)
    return (values - centre) * lax.rsqrt(spread + 1e-05) * gain


def add_rows(left, block_rows):
    return jnp.dot(left, block_rows, preferred_element_type=jnp.float32)


def body(
    frames, segment_ids, ln_attn_gain, w_qkv, w_out, ln_conv_gain, w_glu, dw_kernel, ln_mid_gain
):
    width = HEADS * HD
    local = frames[0]
    frame_count = local.shape[0]
    local_segs = segment_ids[0]
    shard_index = lax.axis_index("seq")
    first_frame = shard_index * frame_count
    all_segs = lax.all_gather(segment_ids, "seq", axis=1, tiled=True)[0]
    normed = layer_norm(local, ln_attn_gain).astype(jnp.bfloat16)
    projected = add_rows(normed, lax.all_gather(w_qkv, "dp", axis=0, tiled=True))
    projected = projected.astype(jnp.bfloat16)
    queries = projected[:, :width].reshape(frame_count, HEADS, HD)
    keys_local = projected[:, width : 2 * width]
    values_local = projected[:, 2 * width :]
    inverse_root = 1.0 / math.sqrt(HD)
    keys_part = lax.all_gather(keys_local, "seq", axis=0, tiled=True)
    values_part = lax.all_gather(values_local, "seq", axis=0, tiled=True)
    rows = keys_part.shape[0]
    running = jnp.full((HEADS, frame_count), -1e30, jnp.float32)
    scores = (
        jnp.einsum(
            "qhd,khd->hqk",
            queries,
            keys_part.reshape(rows, HEADS, HD),
            preferred_element_type=jnp.float32,
        )
        * inverse_root
    )
    same_seg = (local_segs[:, None] == all_segs[None, :])[None]
    scores = jnp.where(same_seg, scores, -1e30)
    newest = jnp.maximum(running, jnp.max(scores, -1))
    raised = jnp.where(same_seg, jnp.exp(scores - newest[:, :, None]), 0.0)
    totals = jnp.sum(raised, -1)
    product = jnp.einsum(
        "hqk,khd->qhd",
        raised.astype(jnp.bfloat16),
        values_part.reshape(rows, HEADS, HD),
        preferred_element_type=jnp.float32,
    )
    summed = product
    running, totals, summed = (newest, totals, summed.reshape(frame_count, width))
    attended = (
        (summed.reshape(frame_count, HEADS, HD) / jnp.transpose(totals)[:, :, None])
        .reshape(frame_count, width)
        .astype(jnp.bfloat16)
    )
    attn = add_rows(attended, lax.all_gather(w_out, "dp", axis=0, tiled=True))
    resid = (local.astype(jnp.float32) + attn).astype(jnp.bfloat16)
    glu_in = layer_norm(resid, ln_conv_gain).astype(jnp.bfloat16)
    glu_out = add_rows(glu_in, lax.all_gather(w_glu, "dp", axis=0, tiled=True))
    gated = (glu_out[:, :D] * jax.nn.sigmoid(glu_out[:, D:])).astype(jnp.bfloat16)
    half_taps = CONV_K // 2
    widened = with_halo(gated, (("seq", 0),), half_taps)
    padded_segs = jnp.pad(all_segs, (half_taps, half_taps), constant_values=-1)
    rim_segs = lax.dynamic_slice_in_dim(padded_segs, first_frame, frame_count + 2 * half_taps)
    conv = jnp.zeros((frame_count, D), jnp.float32)
    for tap_index in range(CONV_K):
        keep = (rim_segs[tap_index : tap_index + frame_count] == local_segs)[:, None]
        shifted = widened[tap_index : tap_index + frame_count].astype(jnp.float32)
        conv = conv + jnp.where(keep, shifted * dw_kernel[tap_index], 0.0)
    middle = layer_norm(conv, ln_mid_gain)
    result = (resid.astype(jnp.float32) + middle * jax.nn.sigmoid(middle)).astype(jnp.bfloat16)
    return result[None]


def solution(mesh):
    return jax.shard_map(
        body,
        mesh=mesh,
        in_specs=(
            P("dp", "seq", None),
            P("dp", "seq"),
            P(),
            P("dp", None),
            P("dp", None),
            P(),
            P("dp", None),
            P(),
            P(),
        ),
        out_specs=P("dp", "seq", None),
        check_vma=False,
    )
```

profile of v0, /device:TPU:39, one launch (start us, length us, event | category | flops | bytes accessed | tf_op | source)
XLA Modules:
  0.0 635.7 jit_solution(8516103408520678854)
XLA Ops:
  6.5 0.7 all-gather.6.cloned.1.call-update
  7.3 1.3 convert_reduce_fusion
  9.0 159.5 %all-gather.6.cloned.1.call-done = bf16[1536,2304]{1,0:T(8,128)(2,1)} async-done(((bf16[96,2304]{1,0:T(8,128)(2,1)}), bf16[1536,2304]{1,0:T(8,128)(2,1)}) %all-gather.6.cloned.1.call-update) | async-done | bytes 7077904 | tf_op jit(solution)/shard_map/all_gather | solution.py:48
  168.5 5.1 convolution_convert_fusion
  173.6 1.0 fusion.70
  174.7 0.7 all-gather.8.cloned.1.call-update
  176.0 0.5 all-gather.14.cloned.1.call-update
  176.6 22.1 %all_gather.22 = s32[1,4096]{1,0:T(1,128)S(1)} all-gather(s32[1,256]{1,0:T(1,128)S(1)} %copy-done.2), channel_id=1, replica_groups=mesh['dp'=16,'seq'=16] {'seq'}, dimensions={1}, use_global_device_ids=true | all-gather | bytes 17408 | tf_op jit(solution)/shard_map/all_gather | solution.py:46
  199.2 0.6 broadcast_compare_fusion
  200.0 43.1 %all-gather.10.cloned.1.call-done = bf16[4096,768]{1,0:T(8,128)(2,1)} async-done(((bf16[256,768]{1,0:T(8,128)(2,1)}), bf16[4096,768]{1,0:T(8,128)(2,1)}) %all-gather.10.cloned.1.call-update) | async-done | bytes 6291472 | tf_op jit(solution)/shard_map/all_gather | solution.py:54
  243.1 8.6 %copy.15 = bf16[4096,768]{0,1:T(8,128)(2,1)} copy(bf16[4096,768]{1,0:T(8,128)(2,1)} %all-gather.10.cloned.1.call-done) | data formatting | bytes 12582912 | tf_op jit(solution)/shard_map/all_gather | solution.py:54
  251.7 61.2 %all-gather.8.cloned.1.call-done = bf16[4096,768]{1,0:T(8,128)(2,1)} async-done(((bf16[256,768]{1,0:T(8,128)(2,1)}), bf16[4096,768]{1,0:T(8,128)(2,1)}) %all-gather.8.cloned.1.call-update) | async-done | bytes 6291472 | tf_op jit(solution)/shard_map/all_gather | solution.py:55
  312.9 8.7 %copy.13 = bf16[4096,768]{0,1:T(8,128)(2,1)} copy(bf16[4096,768]{1,0:T(8,128)(2,1)} %all-gather.8.cloned.1.call-done) | data formatting | bytes 12582912 | tf_op jit(solution)/shard_map/all_gather | solution.py:55
  321.6 23.4 %fusion = (f32[12,256]{1,0:T(8,128)S(1)}, f32[12,256,4096]{2,1,0:T(8,128)}) fusion(pred[256,4096]{1,0:T(8,128)(4,1)S(1)} %broadcast_compare_fusion, bf16[256,12,64]{0,2,1:T(8,128)(2,1)S(1)} %bitcast.41, bf16[4096,12,64]{0,2,1:T(8,128)(2,1)} %bitcast.39), kind=kOutput, calls=%fused_computation.2 | convolution fusion | flops 1648358400 | bytes 58077184 | tf_op jit(solution)/shard_map/qhd,khd->hqk/dot_general | solution.py:59
  345.0 23.5 %fusion.1 = f32[12,256]{1,0:T(8,128)S(1)} fusion(f32[12,256,4096]{2,1,0:T(8,128)} %get-tuple-element.77, f32[12,256]{1,0:T(8,128)S(1)} %broadcast_maximum_fusion, pred[256,4096]{1,0:T(8,128)(4,1)S(1)} %broadcast_compare_fusion), kind=kLoop, calls=%fused_computation.3 | loop fusion | flops 62911488 | bytes 51404800 | tf_op jit(solution)/shard_map/reduce_sum | solution.py:71
  368.5 21.7 %fusion.25 = bf16[256,12,64]{0,2,1:T(8,128)(2,1)S(1)} fusion(bf16[4096,12,64]{0,2,1:T(8,128)(2,1)} %bitcast.40, f32[12,256,4096]{2,1,0:T(8,128)} %get-tuple-element.77, f32[12,256]{1,0:T(8,128)S(1)} %broadcast_maximum_fusion, pred[256,4096]{1,0:T(8,128)(4,1)S(1)} %broadcast_compare_fusion, f32[256,12]{0,1:T(8,128)S(1)} %bitcast.45), kind=kOutput, calls=%fused_computation.62 | convolution fusion | flops 1673920512 | bytes 58089472 | tf_op jit(solution)/shard_map/hqk,khd->qhd/dot_general | solution.py:72
  390.2 2.5 fusion.72
  393.1 199.7 %all-gather.14.cloned.1.call-done = bf16[1536,3072]{1,0:T(8,128)(2,1)} async-done(((bf16[96,3072]{1,0:T(8,128)(2,1)}), bf16[1536,3072]{1,0:T(8,128)(2,1)}) %all-gather.14.cloned.1.call-update) | async-done | bytes 9437200 | tf_op jit(solution)/shard_map/all_gather | solution.py:88
  592.8 5.3 fusion.28
  598.5 4.7 collective-permute-start
  603.2 1.9 collective-permute-start.1
  605.4 5.7 collective-permute-done.1
  611.0 16.3 %fusion.69 = (f32[256]{0:T(256)S(1)}, f32[256,1536]{1,0:T(8,128)S(1)}) fusion(f32[1536]{0:T(1024)S(1)} %get-tuple-element.35, bf16[16,1536]{1,0:T(8,128)(2,1)S(1)} %collective-permute-done.1, bf16[256,1536]{1,0:T(8,128)(2,1)S(1)} %fusion.18, pred[256]{0:T(512)(128)(4,1)S(1)} %get-tuple-element.45, f32[1536]{0:T(1024)S(1)} %get-tuple-element.36, ...), kind=kLoop, calls=%fused_computation.195 | loop fusion | flops 86900480 | bytes 2663424 | tf_op jit(solution)/shard_map/reduce_sum | solution.py:28
  627.6 1.5 fusion.65
  (39 shorter events, 3.1 us)
Async XLA Ops:
  6.5 2.1 copy-start
  6.5 161.9 %copy-start.4 = (f32[1536]{0:T(1024)S(1)}, f32[1536]{0:T(1024)}, u32[]{:S(2)}) copy-start(f32[1536]{0:T(1024)} %param.11) | copy-start | bytes 18436
  6.5 161.9 %all-gather.6.cloned.1.call-start = ((), (), s32[]{:S(2)}) async-start(), calls=%async_computation | async-start | bytes 7520256 | tf_op jit(solution)/shard_map/all_gather | solution.py:48
  7.3 235.9 %all-gather.10.cloned.1.call-start = ((), (), s32[]{:S(2)}) async-start(), calls=%async_computation.2 | async-start | bytes 6684672 | tf_op jit(solution)/shard_map/all_gather | solution.py:54
  173.6 2.9 copy-start.2
  173.6 25.1 %copy-start.1 = (f32[32,1536]{1,0:T(8,128)S(1)}, f32[32,1536]{1,0:T(8,128)}, u32[]{:S(2)}) copy-start(f32[32,1536]{1,0:T(8,128)} %param.16) | copy-start | bytes 589828
  174.6 138.3 %all-gather.8.cloned.1.call-start = ((), (), s32[]{:S(2)}) async-start(), calls=%async_computation.1 | async-start | bytes 6684672 | tf_op jit(solution)/shard_map/all_gather | solution.py:55
  175.4 214.9 %all-gather.12.cloned.1.call-start = ((), (), s32[]{:S(2)}) async-start(), calls=%async_computation.3 | async-start | bytes 2506752 | tf_op jit(solution)/shard_map/all_gather | solution.py:85
  175.9 416.8 %all-gather.14.cloned.1.call-start = ((), (), s32[]{:S(2)}) async-start(), calls=%async_computation.4 | async-start | bytes 10027008 | tf_op jit(solution)/shard_map/all_gather | solution.py:88
  392.8 200.0 %copy-start.5 = (f32[1536]{0:T(1024)S(1)}, f32[1536]{0:T(1024)}, u32[]{:S(2)}) copy-start(f32[1536]{0:T(1024)} %param.14) | copy-start | bytes 18436
  598.5 6.9 %collective-permute-start = (bf16[16,1536]{1,0:T(8,128)(2,1)S(1)}, bf16[16,1536]{1,0:T(8,128)(2,1)S(1)}, u32[]{:S(2)}, u32[]{:S(2)}) collective-permute-start(bf16[16,1536]{1,0:T(8,128)(2,1)S(1)} %get-tuple-element.42), channel_id=1, source_target_pairs={{0,1},{1,2},{2,3},{3,4},{4,5},{5,6},{6,7},{7,8},{8,9},{9,10},{10,1... | collective-permute-start | bytes 147464 | tf_op jit(solution)/shard_map/ppermute | solution.py:18
  603.2 7.8 %collective-permute-start.1 = (bf16[16,1536]{1,0:T(8,128)(2,1)S(1)}, bf16[16,1536]{1,0:T(8,128)(2,1)S(1)}, u32[]{:S(2)}, u32[]{:S(2)}) collective-permute-start(bf16[16,1536]{1,0:T(8,128)(2,1)S(1)} %get-tuple-element.43), channel_id=1, source_target_pairs={{1,0},{2,1},{3,2},{4,3},{5,4},{6,5},{7,6},{8,7},{9,8},{10,9},{11,1... | collective-permute-start | bytes 147464 | tf_op jit(solution)/shard_map/ppermute | solution.py:21
  611.0 16.6 %copy-start.3 = (f32[1536]{0:T(1024)S(1)}, f32[1536]{0:T(1024)}, u32[]{:S(2)}) copy-start(f32[1536]{0:T(1024)} %param.17) | copy-start | bytes 18436
Sparse Core Ops, SparseCore 0:
  9.1 159.2 all-gather.5
  174.8 68.3 all-gather.9
  245.9 66.9 all-gather.7
  314.6 64.0 all-gather.11
  380.3 212.4 all-gather.13
where the time goes:
time: 637 us; the launch traced here: 636 us
  waiting for transfers between devices  472 us (74%)
  matrix products  58 us (9%)
  other arithmetic  44.8 us (7%)
  blocking collectives  22.1 us (3%)
  local copies, waits for them, and re-layouts  19.1 us (3%)
  between operations  13.3 us (2%)
  starting transfers between devices  6.79 us (1%)
    all_gather x1, waiting for transfers between devices, body(): glu_out = add_rows(glu_in, lax.all_gather(w_glu, 'dp', axis=0, tiled=True))  200 us
    all_gather x1, waiting for transfers between devices, body(): lax.all_gather(w_qkv, 'dp', axis=0, tiled=True)  159 us
    all_gather x1, waiting for transfers between devices, body(): values_part = lax.all_gather(values_local, 'seq', axis=0, tiled=True)  61.2 us
    all_gather x1, waiting for transfers between devices, body(): keys_part = lax.all_gather(keys_local, 'seq', axis=0, tiled=True)  43.1 us
    reduce_sum x1, other arithmetic, body(): totals = jnp.sum(raised, -1)  23.5 us
    dot_general x1, matrix products, body(): jnp.einsum('qhd,khd->hqk', queries, keys_part.reshape(rows, HEADS, HD), p...  23.4 us
    all_gather x1, blocking collectives, body(): all_segs = lax.all_gather(segment_ids, 'seq', axis=1, tiled=True)[0]  22.1 us
    dot_general x1, matrix products, body(): jnp.einsum('hqk,khd->qhd', raised.astype(jnp.bfloat16), values_part.resha...  21.7 us
  transfers between devices with their start and end apart: 7, of which 5 were waited for; matrix products, arithmetic and copies ran while one was open for 14% of the time, Pallas kernels for 0%

commit v1 on v0

--- a/solution.py
+++ b/solution.py
@@ -8,6 +8,18 @@
 HEADS = 12
 HD = 64
 CONV_K = 32
+
+
+def pairs_all_find(row_data):
+    return jnp.concatenate(
+        lax.all_to_all(
+            jnp.stack(tuple((row_data for _ in range(lax.axis_size("dp")))), 0),
+            axis_name="dp",
+            split_axis=0,
+            concat_axis=0,
+        ),
+        0,
+    )
 
 
 def with_halo(block, sides, width):
@@ -85,7 +97,7 @@
     attn = add_rows(attended, lax.all_gather(w_out, "dp", axis=0, tiled=True))
     resid = (local.astype(jnp.float32) + attn).astype(jnp.bfloat16)
     glu_in = layer_norm(resid, ln_conv_gain).astype(jnp.bfloat16)
-    glu_out = add_rows(glu_in, lax.all_gather(w_glu, "dp", axis=0, tiled=True))
+    glu_out = add_rows(glu_in, pairs_all_find(w_glu))
     gated = (glu_out[:, :D] * jax.nn.sigmoid(glu_out[:, D:])).astype(jnp.bfloat16)
     half_taps = CONV_K // 2
     widened = with_halo(gated, (("seq", 0),), half_taps)

time: 637 us -> 514 us (0.81)
  waiting for transfers between devices: 472 us -> 316 us
  blocking collectives: 22.1 us -> 34.5 us
  starting transfers between devices: 6.79 us -> 18.9 us
    all_gather x1 -> x0, waiting for transfers between devices: 200 us -> none  [body(): glu_out = add_rows(glu_in, lax.all_gather(w_glu, 'dp', axis=0, tiled=True))]
    all_gather x1, waiting for transfers between devices: 0.02 us -> 53.1 us  [body(): attn = add_rows(attended, lax.all_gather(w_out, 'dp', axis=0, tiled=True))]
    all_gather x1, waiting for transfers between devices: 43.1 us -> 23.7 us  [body(): keys_part = lax.all_gather(keys_local, 'seq', axis=0, tiled=True)]
    all_gather x1, blocking collectives: 22.1 us -> 34.5 us  [body(): all_segs = lax.all_gather(segment_ids, 'seq', axis=1, tiled=True)[0]]
    all_gather x1, waiting for transfers between devices: 61.2 us -> 72.5 us  [body(): values_part = lax.all_gather(values_local, 'seq', axis=0, tiled=True)]
    all_to_all x0 -> x1, starting transfers between devices: none -> 6.99 us  [pairs_all_find(): lax.all_to_all(jnp.stack(tuple((row_data for _ in range(lax.axis_size('dp...]
  transfers between devices with their start and end apart: 7 -> 7, of which waited for: 5 -> 5; matrix products, arithmetic and copies ran while one was open for 14% -> 19% of each run, Pallas kernels for 0% -> 0%
where the time goes in v1:
time: 514 us; the launch traced here: 510 us
  waiting for transfers between devices  316 us (61%)
  matrix products  57.8 us (11%)
  other arithmetic  45.1 us (9%)
  blocking collectives  34.5 us (7%)
  local copies, waits for them, and re-layouts  24.2 us (5%)
  starting transfers between devices  18.9 us (4%)
  between operations  13.3 us (3%)
    all_gather x1, waiting for transfers between devices, body(): lax.all_gather(w_qkv, 'dp', axis=0, tiled=True)  159 us
    all_gather x1, waiting for transfers between devices, body(): values_part = lax.all_gather(values_local, 'seq', axis=0, tiled=True)  72.5 us
    all_gather x1, waiting for transfers between devices, body(): attn = add_rows(attended, lax.all_gather(w_out, 'dp', axis=0, tiled=True))  53.1 us
    all_gather x1, blocking collectives, body(): all_segs = lax.all_gather(segment_ids, 'seq', axis=1, tiled=True)[0]  34.5 us
    reduce_sum x1, other arithmetic, body(): totals = jnp.sum(raised, -1)  23.8 us
    all_gather x1, waiting for transfers between devices, body(): keys_part = lax.all_gather(keys_local, 'seq', axis=0, tiled=True)  23.7 us
    dot_general x1, matrix products, body(): jnp.einsum('qhd,khd->hqk', queries, keys_part.reshape(rows, HEADS, HD), p...  23.3 us
    dot_general x1, matrix products, body(): jnp.einsum('hqk,khd->qhd', raised.astype(jnp.bfloat16), values_part.resha...  21.6 us
  transfers between devices with their start and end apart: 7, of which 5 were waited for; matrix products, arithmetic and copies ran while one was open for 19% of the time, Pallas kernels for 0%

profile of v1, /device:TPU:39, one launch (start us, length us, event | category | flops | bytes accessed | tf_op | source)
XLA Modules:
  0.0 510.3 jit_solution(12276052029095379538)
XLA Ops:
  6.5 0.7 all-gather.5.cloned.1.call-update
  7.3 1.3 convert_reduce_fusion
  9.0 159.5 %all-gather.5.cloned.1.call-done = bf16[1536,2304]{1,0:T(8,128)(2,1)} async-done(((bf16[96,2304]{1,0:T(8,128)(2,1)}), bf16[1536,2304]{1,0:T(8,128)(2,1)}) %all-gather.5.cloned.1.call-update) | async-done | bytes 7077904 | tf_op jit(solution)/shard_map/all_gather | solution.py:60
  168.5 5.1 %convolution_convert_fusion = bf16[256,2304]{1,0:T(8,128)(2,1)S(1)} fusion(bf16[1536,2304]{1,0:T(8,128)(2,1)} %all-gather.5.cloned.1.call-done, bf16[1,256,1536]{2,1,0:T(8,128)(2,1)S(1)} %copy-done, f32[1536]{0:T(1024)S(1)} %copy-done.5, f32[256]{0:T(256)S(1)} %add_rsqrt_fusion.2, f32[256]{0:T(256)S(1)} %broadcast_multiply_fusion.2), kind=kOutput, calls=%fused_computation.36 | convolution fusion | flops 1814495232 | bytes 9052160 | tf_op jit(solution)/shard_map/dot_general | solution.py:46
  173.6 1.0 fusion.70
  174.7 0.7 all-gather.7.cloned.1.call-update
  175.4 4.8 stack.2
  180.1 7.0 %all-to-all-start = ((bf16[16,96,3072]{2,1,0:T(8,128)(2,1)}), bf16[16,96,3072]{2,1,0:T(8,128)(2,1)}, u32[]{:S(2)}, u32[]{:S(2)}) async-start(bf16[16,96,3072]{2,1,0:T(8,128)(2,1)} %stack.2), calls=%async_computation | async-start | bytes 18874368 | tf_op jit(solution)/shard_map/all_to_all | solution.py:15
  187.7 34.5 %all_gather.19 = s32[1,4096]{1,0:T(1,128)S(1)} all-gather(s32[1,256]{1,0:T(1,128)S(1)} %copy-done.3), channel_id=1, replica_groups=mesh['dp'=16,'seq'=16] {'seq'}, dimensions={1}, use_global_device_ids=true | all-gather | bytes 17408 | tf_op jit(solution)/shard_map/all_gather | solution.py:58
  223.6 23.7 %all-gather.9.cloned.1.call-done = bf16[4096,768]{1,0:T(8,128)(2,1)} async-done(((bf16[256,768]{1,0:T(8,128)(2,1)}), bf16[4096,768]{1,0:T(8,128)(2,1)}) %all-gather.9.cloned.1.call-update) | async-done | bytes 6291472 | tf_op jit(solution)/shard_map/all_gather | solution.py:66
  247.3 8.6 %copy.15 = bf16[4096,768]{0,1:T(8,128)(2,1)} copy(bf16[4096,768]{1,0:T(8,128)(2,1)} %all-gather.9.cloned.1.call-done) | data formatting | bytes 12582912 | tf_op jit(solution)/shard_map/all_gather | solution.py:66
  255.9 23.3 %fusion = (f32[12,256]{1,0:T(8,128)S(1)}, f32[12,256,4096]{2,1,0:T(8,128)}) fusion(pred[256,4096]{1,0:T(8,128)(4,1)S(1)} %broadcast_compare_fusion, bf16[256,12,64]{0,2,1:T(8,128)(2,1)S(1)} %bitcast.42, bf16[4096,12,64]{0,2,1:T(8,128)(2,1)} %bitcast.40), kind=kOutput, calls=%fused_computation.2 | convolution fusion | flops 1648358400 | bytes 58077184 | tf_op jit(solution)/shard_map/qhd,khd->hqk/dot_general | solution.py:71
  279.2 23.8 %fusion.1 = f32[12,256]{1,0:T(8,128)S(1)} fusion(f32[12,256,4096]{2,1,0:T(8,128)} %get-tuple-element.77, f32[12,256]{1,0:T(8,128)S(1)} %broadcast_maximum_fusion, pred[256,4096]{1,0:T(8,128)(4,1)S(1)} %broadcast_compare_fusion), kind=kLoop, calls=%fused_computation.3 | loop fusion | flops 62911488 | bytes 51404800 | tf_op jit(solution)/shard_map/reduce_sum | solution.py:83
  303.0 72.5 %all-gather.7.cloned.1.call-done = bf16[4096,768]{1,0:T(8,128)(2,1)} async-done(((bf16[256,768]{1,0:T(8,128)(2,1)}), bf16[4096,768]{1,0:T(8,128)(2,1)}) %all-gather.7.cloned.1.call-update) | async-done | bytes 6291472 | tf_op jit(solution)/shard_map/all_gather | solution.py:67
  375.6 8.6 %copy.13 = bf16[4096,768]{0,1:T(8,128)(2,1)} copy(bf16[4096,768]{1,0:T(8,128)(2,1)} %all-gather.7.cloned.1.call-done) | data formatting | bytes 12582912 | tf_op jit(solution)/shard_map/all_gather | solution.py:67
  384.2 21.6 %fusion.25 = bf16[256,12,64]{0,2,1:T(8,128)(2,1)S(1)} fusion(bf16[4096,12,64]{0,2,1:T(8,128)(2,1)} %bitcast.41, f32[12,256,4096]{2,1,0:T(8,128)} %get-tuple-element.77, f32[12,256]{1,0:T(8,128)S(1)} %broadcast_maximum_fusion, pred[256,4096]{1,0:T(8,128)(4,1)S(1)} %broadcast_compare_fusion, f32[256,12]{0,1:T(8,128)S(1)} %bitcast.46), kind=kOutput, calls=%fused_computation.62 | convolution fusion | flops 1673920512 | bytes 58089472 | tf_op jit(solution)/shard_map/hqk,khd->qhd/dot_general | solution.py:84
  405.9 53.1 %all-gather.11.cloned.1.call-done = bf16[768,1536]{1,0:T(8,128)(2,1)} async-done(((bf16[48,1536]{1,0:T(8,128)(2,1)}), bf16[768,1536]{1,0:T(8,128)(2,1)}) %all-gather.11.cloned.1.call-update) | async-done | bytes 2359312 | tf_op jit(solution)/shard_map/all_gather | solution.py:97
  458.9 2.5 fusion.72
  462.2 5.2 %fusion.28 = f32[256,3072]{1,0:T(8,128)S(1)} fusion(bf16[1536,3072]{1,0:T(8,128)(2,1)} %bitcast.9, f32[256,1536]{1,0:T(8,128)S(1)} %get-tuple-element.79, f32[1536]{0:T(1024)S(1)} %copy-done.6, f32[256]{0:T(256)S(1)} %add_rsqrt_fusion.1, f32[256]{0:T(256)S(1)} %broadcast_multiply_fusion.1), kind=kOutput, calls=%fused_computation.63 | convolution fusion | flops 2417491968 | bytes 14163968 | tf_op jit(solution)/shard_map/dot_general | solution.py:46
  467.9 9.9 %collective-permute-start = (bf16[16,1536]{1,0:T(8,128)(2,1)S(1)}, bf16[16,1536]{1,0:T(8,128)(2,1)S(1)}, u32[]{:S(2)}, u32[]{:S(2)}) collective-permute-start(bf16[16,1536]{1,0:T(8,128)(2,1)S(1)} %get-tuple-element.42), channel_id=1, source_target_pairs={{0,1},{1,2},{2,3},{3,4},{4,5},{5,6},{6,7},{7,8},{8,9},{9,10},{10,1... | collective-permute-start | bytes 147464 | tf_op jit(solution)/shard_map/ppermute | solution.py:30
  477.8 1.9 collective-permute-start.1
  479.9 5.7 %collective-permute-done.1 = bf16[16,1536]{1,0:T(8,128)(2,1)S(1)} collective-permute-done((bf16[16,1536]{1,0:T(8,128)(2,1)S(1)}, bf16[16,1536]{1,0:T(8,128)(2,1)S(1)}, u32[]{:S(2)}, u32[]{:S(2)}) %collective-permute-start.1) | collective-permute-done | bytes 49184 | tf_op jit(solution)/shard_map/ppermute | solution.py:33
  485.6 16.3 %fusion.69 = (f32[256]{0:T(256)S(1)}, f32[256,1536]{1,0:T(8,128)S(1)}) fusion(f32[1536]{0:T(1024)S(1)} %get-tuple-element.35, bf16[16,1536]{1,0:T(8,128)(2,1)S(1)} %collective-permute-done.1, bf16[256,1536]{1,0:T(8,128)(2,1)S(1)} %fusion.18, pred[256]{0:T(512)(128)(4,1)S(1)} %get-tuple-element.45, f32[1536]{0:T(1024)S(1)} %get-tuple-element.36, ...), kind=kLoop, calls=%fused_computation.195 | loop fusion | flops 86900480 | bytes 2663424 | tf_op jit(solution)/shard_map/reduce_sum | solution.py:40
  502.2 1.5 fusion.65
  (41 shorter events, 4.1 us)
Async XLA Ops:
  6.5 2.1 copy-start
  6.5 161.9 %copy-start.5 = (f32[1536]{0:T(1024)S(1)}, f32[1536]{0:T(1024)}, u32[]{:S(2)}) copy-start(f32[1536]{0:T(1024)} %param.11) | copy-start | bytes 18436
  6.5 161.9 %all-gather.5.cloned.1.call-start = ((), (), s32[]{:S(2)}) async-start(), calls=%async_computation.1 | async-start | bytes 7520256 | tf_op jit(solution)/shard_map/all_gather | solution.py:60
  7.3 240.0 %all-gather.9.cloned.1.call-start = ((), (), s32[]{:S(2)}) async-start(), calls=%async_computation.3 | async-start | bytes 6684672 | tf_op jit(solution)/shard_map/all_gather | solution.py:66
  173.6 1.7 copy-start.1
  174.6 201.0 %all-gather.7.cloned.1.call-start = ((), (), s32[]{:S(2)}) async-start(), calls=%async_computation.2 | async-start | bytes 6684672 | tf_op jit(solution)/shard_map/all_gather | solution.py:67
  180.1 7.6 %copy-start.3 = (s32[1,256]{1,0:T(1,128)S(1)}, s32[1,256]{1,0:T(1,128)}, u32[]{:S(2)}) copy-start(s32[1,256]{1,0:T(1,128)} %param.10) | copy-start | bytes 3076
  180.1 42.1 %copy-start.2 = (f32[32,1536]{1,0:T(8,128)S(1)}, f32[32,1536]{1,0:T(8,128)}, u32[]{:S(2)}) copy-start(f32[32,1536]{1,0:T(8,128)} %param.16) | copy-start | bytes 589828
  180.1 281.7 %all-to-all-start = ((bf16[16,96,3072]{2,1,0:T(8,128)(2,1)}), bf16[16,96,3072]{2,1,0:T(8,128)(2,1)}, u32[]{:S(2)}, u32[]{:S(2)}) async-start(bf16[16,96,3072]{2,1,0:T(8,128)(2,1)} %stack.2), calls=%async_computation | async-start | bytes 18874368 | tf_op jit(solution)/shard_map/all_to_all | solution.py:15
  187.1 271.8 %all-gather.11.cloned.1.call-start = ((), (), s32[]{:S(2)}) async-start(), calls=%async_computation.4 | async-start | bytes 2506752 | tf_op jit(solution)/shard_map/all_gather | solution.py:97
  461.5 0.7 copy-start.6
  467.9 12.1 %collective-permute-start = (bf16[16,1536]{1,0:T(8,128)(2,1)S(1)}, bf16[16,1536]{1,0:T(8,128)(2,1)S(1)}, u32[]{:S(2)}, u32[]{:S(2)}) collective-permute-start(bf16[16,1536]{1,0:T(8,128)(2,1)S(1)} %get-tuple-element.42), channel_id=1, source_target_pairs={{0,1},{1,2},{2,3},{3,4},{4,5},{5,6},{6,7},{7,8},{8,9},{9,10},{10,1... | collective-permute-start | bytes 147464 | tf_op jit(solution)/shard_map/ppermute | solution.py:30
  477.8 7.8 %collective-permute-start.1 = (bf16[16,1536]{1,0:T(8,128)(2,1)S(1)}, bf16[16,1536]{1,0:T(8,128)(2,1)S(1)}, u32[]{:S(2)}, u32[]{:S(2)}) collective-permute-start(bf16[16,1536]{1,0:T(8,128)(2,1)S(1)} %get-tuple-element.43), channel_id=1, source_target_pairs={{1,0},{2,1},{3,2},{4,3},{5,4},{6,5},{7,6},{8,7},{9,8},{10,9},{11,1... | collective-permute-start | bytes 147464 | tf_op jit(solution)/shard_map/ppermute | solution.py:33
  485.6 16.6 %copy-start.4 = (f32[1536]{0:T(1024)S(1)}, f32[1536]{0:T(1024)}, u32[]{:S(2)}) copy-start(f32[1536]{0:T(1024)} %param.17) | copy-start | bytes 18436
Sparse Core Ops, SparseCore 0:
  9.1 159.2 all-gather.4
  174.7 72.5 all-gather.8
  250.1 125.4 all-gather.6
  377.2 81.6 all-gather.10
